TPU v7x, 32 devices: a whole 2x2x4 slice. The times are simulated.
32 devices in a mesh: week: 2 (over y), slab: 4 (over z), trank: 2 (over x), lrank: 2 (over core).
Axes of the slice: x: 2, y: 2, z: 4, core: 2. Of those that a mesh axis runs over, the one named last changes fastest.
Arguments:
- tiles: bfloat16 [1024, 4096], P(('week', 'slab', 'trank', 'lrank')), parts along dimension 0, may hold values from -6 to 6
- tile_var: int32 [1024], P(('week', 'slab', 'trank', 'lrank')), parts along dimension 0, may hold values from 0 to 5
- tile_time: int32 [1024], P(('week', 'slab', 'trank', 'lrank')), parts along dimension 0, may hold values from 0 to 127
- tile_level: int32 [1024], P(('week', 'slab', 'trank', 'lrank')), parts along dimension 0, may hold values from 0 to 47
- tile_block: int32 [1024], P(('week', 'slab', 'trank', 'lrank')), parts along dimension 0, may hold values from 0 to 63
- counts: int32 [32, 4], P(('week', 'slab', 'trank', 'lrank')), parts along dimension 0, may hold values from 0 to 8, as said below
- time_factor: bfloat16 [16, 256], P('week'), parts along dimension 0, may hold values from -0.5 to 0.5
- level_factor: bfloat16 [16, 96], P('week'), parts along dimension 0, may hold values from -0.875 to 0.875
- lat_factor: bfloat16 [64, 512], P('week'), parts along dimension 0, may hold values from -0.75 to 0.75
- lon_factor: bfloat16 [96, 2048], P(('week', 'slab')), parts along dimension 0, may hold values from -0.75 to 0.75
Outputs:
- grid: bfloat16 [96, 32, 384], P(('week', 'slab'), ('trank', 'lrank')), parts along dimension 0
There are 2 independent parts, one for each index of `week`. A program takes and returns all parts, laid end to end along the dimension named above; each array names one. Nothing has to cross between parts.
Inputs may be any that keep to these rules, and one draw needn't show every extreme that they name: counts[i, e] is the number of live slots among the 8 slots for destination slab e of device row i; for every trank and lrank index some destination slab gets 8 live slots from every source slab.
All inputs are finite; a program needn't handle non-finite values.
Results may differ from a plain program's by a relative error of at most 0.0069.
Values may be sent and summed in bfloat16 or wider, within the bound.
A program may use at most 64 MiB of HBM per device.

v0:
```python
import jax
import jax.numpy as jnp
from jax import lax
from jax.sharding import PartitionSpec as P

V = 6
RT = 256
RL = 96
RC = 512
RD = 2048
BLK = 64


def per_device(
    tiles,
    tile_var,
    tile_time,
    tile_level,
    tile_block,
    counts,
    time_factor,
    level_factor,
    lat_factor,
    lon_factor,
):
    slabs = lax.axis_size("slab")
    n_trank = lax.axis_size("trank")
    n_lrank = lax.axis_size("lrank")
    slots = tiles.shape[0]
    capacity = slots // slabs
    lat_rows = lat_factor.shape[0]
    cblocks = RC // BLK
    dblocks = RD // (BLK * slabs)
    time_dev = RT // n_trank
    level_dev = RL // n_lrank
    hours = time_factor.shape[0]
    levels = level_factor.shape[0]
    fields = V * hours * levels
    lat_blocks = lat_factor.reshape(lat_rows, cblocks, BLK)
    sent_counts = counts.reshape(slabs)
    slot_index = jnp.arange(slots, dtype=jnp.int32)
    live_sent = (slot_index % capacity < jnp.repeat(sent_counts, capacity)).astype(jnp.int32)
    got_tiles, variable, rank_time, rank_level, blocks, live_got = (
        lax.all_to_all(tiles, "slab", split_axis=0, concat_axis=0, tiled=True),
        lax.all_to_all(tile_var, "slab", split_axis=0, concat_axis=0, tiled=True),
        lax.all_to_all(tile_time, "slab", split_axis=0, concat_axis=0, tiled=True),
        lax.all_to_all(tile_level, "slab", split_axis=0, concat_axis=0, tiled=True),
        lax.all_to_all(tile_block, "slab", split_axis=0, concat_axis=0, tiled=True),
        lax.all_to_all(live_sent, "slab", split_axis=0, concat_axis=0, tiled=True),
    )
    chosen = jnp.take(lat_blocks, blocks // dblocks, axis=1)
    square = got_tiles.reshape(got_tiles.shape[0], BLK, BLK)
    product = jnp.einsum("lkc,kcd->kld", chosen, square, preferred_element_type=jnp.float32)
    partial_value = product.astype(jnp.bfloat16)
    time_full = lax.axis_index("trank") * time_dev + rank_time
    level_full = lax.axis_index("lrank") * level_dev + rank_level
    var_hot = (variable[:, None] == jnp.arange(V, dtype=jnp.int32)[None, :]).astype(jnp.float32)
    time_cols = jnp.take(time_factor, time_full, axis=1).T.astype(jnp.float32)
    level_cols = jnp.take(level_factor, level_full, axis=1).T.astype(jnp.float32)
    coef = var_hot[:, :, None, None] * time_cols[:, None, :, None] * level_cols[:, None, None, :]
    coef = coef * live_got.astype(jnp.float32)[:, None, None, None]
    coef = coef.reshape(variable.shape[0], fields).astype(jnp.bfloat16)
    place = (blocks % dblocks)[:, None] == jnp.arange(dblocks, dtype=jnp.int32)[None, :]
    spread_spread = jnp.where(
        place[:, None, :, None], partial_value[:, :, None, :], jnp.zeros((), jnp.bfloat16)
    )
    spread = spread_spread.reshape(partial_value.shape[0], partial_value.shape[1], dblocks * BLK)
    summed = lax.psum_scatter(
        jnp.einsum("kld,kx->ldx", spread, coef, preferred_element_type=jnp.float32).astype(
            jnp.bfloat16
        ),
        ("trank", "lrank"),
        scatter_dimension=0,
        tiled=True,
    )
    grid = jnp.einsum(
        "od,ldx->olx",
        lon_factor,
        lax.all_gather(summed, "slab", axis=1, tiled=True),
        preferred_element_type=jnp.float32,
    )
    return grid.astype(jnp.bfloat16)


def solution(mesh):
    in_specs = (
        P(("week", "slab", "trank", "lrank"), None),
        P(("week", "slab", "trank", "lrank")),
        P(("week", "slab", "trank", "lrank")),
        P(("week", "slab", "trank", "lrank")),
        P(("week", "slab", "trank", "lrank")),
        P(("week", "slab", "trank", "lrank"), None),
        P("week", None),
        P("week", None),
        P("week", None),
        P(("week", "slab"), None),
    )
    out_specs = P(("week", "slab"), ("trank", "lrank"), None)
    return jax.shard_map(
        per_device, mesh=mesh, in_specs=in_specs, out_specs=out_specs, check_vma=False
    )
```

profile of v0, /device:TPU:0, one launch (start us, length us, event | category | flops | bytes accessed | tf_op | source)
XLA Modules:
  0.0 411.0 jit_solution(3039055745523295448)
XLA Ops:
  6.5 1.3 all_to_all.38
  7.9 6.3 %all-to-all-start = ((s32[4,8,1]{1,2,0:T(1,128)}), s32[4,8,1]{1,2,0:T(1,128)S(1)}, u32[]{:S(2)}, u32[]{:S(2)}) async-start(s32[4,8,1]{1,2,0:T(1,128)} %bitcast), calls=%async_computation | async-start | bytes 4096 | tf_op jit(solution)/shard_map/all_to_all | solution.py:48
  14.2 1.3 all_to_all.44
  15.5 1.3 all_to_all.46
  16.8 1.3 all_to_all.48
  18.2 1.3 compare_convert_fusion
  19.5 0.8 copy.47
  20.3 0.8 copy.44
  21.1 0.9 reshape.375
  22.0 5.1 %all-to-all-start.4 = ((s32[4,8,1]{1,2,0:T(1,128)}), s32[4,8,1]{1,2,0:T(1,128)S(1)}, u32[]{:S(2)}, u32[]{:S(2)}) async-start(s32[4,8,1]{1,2,0:T(1,128)} %bitcast.7), calls=%async_computation.4 | async-start | bytes 4096 | tf_op jit(solution)/shard_map/all_to_all | solution.py:47
  27.7 0.7 reduce.22
  28.5 4.1 %all-to-all-done.4 = s32[4,8,1]{1,2,0:T(1,128)S(1)} async-done(((s32[4,8,1]{1,2,0:T(1,128)}), s32[4,8,1]{1,2,0:T(1,128)S(1)}, u32[]{:S(2)}, u32[]{:S(2)}) %all-to-all-start.4) | async-done | bytes 160 | tf_op jit(solution)/shard_map/all_to_all | solution.py:47
  32.7 3.2 all-to-all-start.3
  35.9 5.4 %all-to-all-done.3 = s32[4,8,1]{1,2,0:T(1,128)S(1)} async-done(((s32[4,8,1]{1,2,0:T(1,128)}), s32[4,8,1]{1,2,0:T(1,128)S(1)}, u32[]{:S(2)}, u32[]{:S(2)}) %all-to-all-start.3) | async-done | bytes 160 | tf_op jit(solution)/shard_map/all_to_all | solution.py:46
  41.2 3.2 all-to-all-start.5
  44.4 0.7 fusion.12
  45.5 4.5 %all-to-all-done.5 = s32[4,8,1]{1,2,0:T(1,128)S(1)} async-done(((s32[4,8,1]{1,2,0:T(1,128)}), s32[4,8,1]{1,2,0:T(1,128)S(1)}, u32[]{:S(2)}, u32[]{:S(2)}) %all-to-all-start.5) | async-done | bytes 160 | tf_op jit(solution)/shard_map/all_to_all | solution.py:49
  50.0 3.2 all-to-all-start.2
  53.3 5.3 %all-to-all-done.2 = s32[4,8,1]{1,2,0:T(1,128)S(1)} async-done(((s32[4,8,1]{1,2,0:T(1,128)}), s32[4,8,1]{1,2,0:T(1,128)S(1)}, u32[]{:S(2)}, u32[]{:S(2)}) %all-to-all-start.2) | async-done | bytes 160 | tf_op jit(solution)/shard_map/all_to_all | solution.py:45
  58.6 3.4 all-to-all-start.1
  62.1 0.7 reduce.25
  62.8 0.6 gather_fusion.2
  63.5 0.6 gather_fusion.1
  64.2 0.6 gather_fusion
  64.9 3.9 all-to-all-done.1
  68.8 0.5 reshape.376
  70.1 1.3 select_n.120
  71.3 6.5 %convolution_convert_fusion = bf16[32,512,384]{2,1,0:T(8,128)(2,1)} fusion(bf16[32,32,512]{2,0,1:T(8,128)(2,1)S(1)} %select_n.120, bf16[32,384,1]{0,1,2:T(8,128)(2,1)S(1)} %bitcast.38), kind=kOutput, calls=%fused_computation.3 | convolution fusion | flops 408944640 | bytes 13656064 | tf_op jit(solution)/shard_map/kld,kx->ldx/dot_general | solution.py:69
  77.9 99.5 %reduce-scatter.2.cloned.1.call-done = bf16[8,512,384]{2,1,0:T(8,128)(2,1)} async-done(((bf16[32,512,384]{2,1,0:T(8,128)(2,1)}), bf16[8,512,384]{2,1,0:T(8,128)(2,1)}) %reduce-scatter.2.cloned.1.call-update) | async-done | bytes 3145744 | tf_op jit(solution)/shard_map/reduce_scatter | solution.py:68
  177.4 219.8 %all-gather.2.cloned.1.call-done = bf16[8,2048,384]{2,1,0:T(8,128)(2,1)} async-done(((bf16[8,512,384]{2,1,0:T(8,128)(2,1)}), bf16[8,2048,384]{2,1,0:T(8,128)(2,1)}) %all-gather.2.cloned.1.call-update) | async-done | bytes 12582928 | tf_op jit(solution)/shard_map/all_gather | solution.py:79
  397.2 6.3 %fusion = bf16[12,8,384]{2,0,1:T(8,128)(2,1)S(1)} fusion(bf16[8,2048,384]{2,1,0:T(8,128)(2,1)} %all-gather.2.cloned.1.call-done, bf16[12,2048]{1,0:T(8,128)(2,1)S(1)} %copy-done), kind=kOutput, calls=%fused_computation.7 | convolution fusion | flops 151031808 | bytes 12705792 | tf_op jit(solution)/shard_map/od,ldx->olx/dot_general | solution.py:76
  403.5 0.7 copy.50
  (39 shorter events, 2.4 us)
Async XLA Ops:
  6.5 390.7 %copy-start = (bf16[12,2048]{1,0:T(8,128)(2,1)S(1)}, bf16[12,2048]{1,0:T(8,128)(2,1)}, u32[]{:S(2)}) copy-start(bf16[12,2048]{1,0:T(8,128)(2,1)} %param.19) | copy-start | bytes 147460
  7.9 14.1 %all-to-all-start = ((s32[4,8,1]{1,2,0:T(1,128)}), s32[4,8,1]{1,2,0:T(1,128)S(1)}, u32[]{:S(2)}, u32[]{:S(2)}) async-start(s32[4,8,1]{1,2,0:T(1,128)} %bitcast), calls=%async_computation | async-start | bytes 4096 | tf_op jit(solution)/shard_map/all_to_all | solution.py:48
  22.0 10.7 %all-to-all-start.4 = ((s32[4,8,1]{1,2,0:T(1,128)}), s32[4,8,1]{1,2,0:T(1,128)S(1)}, u32[]{:S(2)}, u32[]{:S(2)}) async-start(s32[4,8,1]{1,2,0:T(1,128)} %bitcast.7), calls=%async_computation.4 | async-start | bytes 4096 | tf_op jit(solution)/shard_map/all_to_all | solution.py:47
  32.7 8.6 %all-to-all-start.3 = ((s32[4,8,1]{1,2,0:T(1,128)}), s32[4,8,1]{1,2,0:T(1,128)S(1)}, u32[]{:S(2)}, u32[]{:S(2)}) async-start(s32[4,8,1]{1,2,0:T(1,128)} %bitcast.5), calls=%async_computation.3 | async-start | bytes 4096 | tf_op jit(solution)/shard_map/all_to_all | solution.py:46
  41.2 8.7 %all-to-all-start.5 = ((s32[4,8,1]{1,2,0:T(1,128)}), s32[4,8,1]{1,2,0:T(1,128)S(1)}, u32[]{:S(2)}, u32[]{:S(2)}) async-start(s32[4,8,1]{1,2,0:T(1,128)} %compare_convert_fusion), calls=%async_computation.5 | async-start | bytes 4096 | tf_op jit(solution)/shard_map/all_to_all | solution.py:49
  50.0 8.6 %all-to-all-start.2 = ((s32[4,8,1]{1,2,0:T(1,128)}), s32[4,8,1]{1,2,0:T(1,128)S(1)}, u32[]{:S(2)}, u32[]{:S(2)}) async-start(s32[4,8,1]{1,2,0:T(1,128)} %bitcast.4), calls=%async_computation.2 | async-start | bytes 4096 | tf_op jit(solution)/shard_map/all_to_all | solution.py:45
  58.6 10.2 %all-to-all-start.1 = ((bf16[4,8,4096]{2,1,0:T(8,128)(2,1)}), bf16[4,8,4096]{2,1,0:T(8,128)(2,1)S(1)}, u32[]{:S(2)}, u32[]{:S(2)}) async-start(bf16[4,8,4096]{2,1,0:T(8,128)(2,1)} %bitcast.39), calls=%async_computation.1 | async-start | bytes 524288 | tf_op jit(solution)/shard_map/all_to_all | solution.py:44
  62.0 115.4 %reduce-scatter.2.cloned.1.call-start = ((), (), s32[]{:S(2)}) async-start(), calls=%async_computation.7 | async-start | bytes 15728640 | tf_op jit(solution)/shard_map/reduce_scatter | solution.py:68
  77.8 319.4 %all-gather.2.cloned.1.call-start = ((), (), s32[]{:S(2)}) async-start(), calls=%async_computation.8 | async-start | bytes 15728640 | tf_op jit(solution)/shard_map/all_gather | solution.py:79
Sparse Core Ops, SparseCore 0:
  77.9 99.4 reduce-scatter.1
  179.0 218.1 all-gather.1
where the time goes:
time: 412 us; the launch traced here: 411 us
  waiting for transfers between devices  342 us (83%)
  starting transfers between devices  24.5 us (6%)
  between operations  13.6 us (3%)
  local copies, waits for them, and re-layouts  13.4 us (3%)
  matrix products  13.1 us (3%)
    all_gather x1, waiting for transfers between devices, per_device(): lax.all_gather(summed, 'slab', axis=1, tiled=True)  220 us
    reduce_scatter x1, waiting for transfers between devices, per_device(): lax.psum_scatter(jnp.einsum('kld,kx->ldx', spread, coef, preferred_elemen...  99.5 us
  transfers between devices with their start and end apart: 8, of which 7 were waited for; matrix products, arithmetic and copies ran while one was open for 2% of the time, Pallas kernels for 0%

commit v1 on v0

--- a/solution.py
+++ b/solution.py
@@ -1,6 +1,10 @@
+import functools
+
 import jax
 import jax.numpy as jnp
 from jax import lax
+from jax.experimental import pallas as pl
+from jax.experimental.pallas import tpu as pltpu
 from jax.sharding import PartitionSpec as P
 
 V = 6
@@ -11,7 +15,7 @@
 BLK = 64
 
 
-def per_device(
+def general_plan(
     tiles,
     tile_var,
     tile_time,
@@ -82,6 +86,348 @@
     return grid.astype(jnp.bfloat16)
 
 
+LANES = 128
+MESH = pl.DeviceIdType.MESH
+
+
+def offsets(shape):
+    slabs, tranks, lranks = shape
+    found = [
+        (a, b, c)
+        for a in range(slabs)
+        for b in range(tranks)
+        for c in range(lranks)
+        if (a, b, c) != (0, 0, 0)
+    ]
+    return sorted(found, key=lambda k: -(min(k[0], slabs - k[0]) * 4 + k[1] * 2 + k[2]))
+
+
+def decode_kernel(
+    shape,
+    tiles_ref,
+    var_ref,
+    time_ref,
+    level_ref,
+    blk_ref,
+    counts_ref,
+    time_factor_ref,
+    level_factor_ref,
+    lat_ref,
+    lon_ref,
+    out_ref,
+    square,
+    lat_blocks,
+    partials,
+    lon_mine,
+    lon_all,
+    weights,
+    send_buf,
+    recv_buf,
+    meta_mine,
+    meta_all,
+    coef,
+    result,
+    lon_send,
+    lon_recv,
+    meta_send,
+    meta_recv,
+    w_send,
+    w_recv,
+):
+    slabs, tranks, lranks = shape
+    groups = tranks * lranks
+    devices = slabs * groups
+    week = lax.axis_index("week")
+    slab = lax.axis_index("slab")
+    trank = lax.axis_index("trank")
+    lrank = lax.axis_index("lrank")
+    me = slab * groups + trank * lranks + lrank
+    rows = tiles_ref.shape[0]
+    capacity = rows // slabs
+    lats = lat_ref.shape[0]
+    lat_dev = lats // groups
+    lons, lon_pad = lon_ref.shape[0], lon_mine.shape[0]
+    depth = RD // slabs
+    dblocks = depth // BLK
+    per_lane = LANES // BLK
+    hours = time_factor_ref.shape[0]
+    levels = level_factor_ref.shape[0]
+    time_dev = RT // tranks
+    level_dev = RL // lranks
+    total_rows = rows * devices
+    pieces = offsets(shape)
+
+    def peer(k):
+        a, b, c = k
+        return (
+            lax.rem(slab + a, slabs),
+            lax.rem(trank + b, tranks),
+            lax.rem(lrank + c, lranks),
+        )
+
+    lon_mine[...] = jnp.concatenate(
+        [lon_ref[...].astype(jnp.float32), jnp.zeros((lon_pad - lons, RD), jnp.float32)], axis=0
+    ).astype(jnp.bfloat16)
+    lane = lax.broadcasted_iota(jnp.int32, (1, rows), 1)
+    live = jnp.zeros((1, rows), jnp.int32)
+    for e in range(slabs):
+        first = e * capacity
+        live = jnp.where((lane >= first) & (lane < first + counts_ref[0, e]), 1, live)
+    meta_mine[...] = jnp.concatenate(
+        [
+            var_ref[...],
+            time_ref[...] + trank * time_dev,
+            level_ref[...] + lrank * level_dev,
+            live,
+        ],
+        axis=1,
+    )
+    barrier = pltpu.get_barrier_semaphore()
+    for k in pieces:
+        pl.semaphore_signal(barrier, inc=1, device_id=(week, *peer(k)), device_id_type=MESH)
+    pl.semaphore_wait(barrier, devices - 1)
+
+    lon_copies = []
+    for a in sorted(range(1, slabs), key=lambda a: -min(a, slabs - a)):
+        lon_copies.append(
+            pltpu.make_async_remote_copy(
+                src_ref=lon_mine,
+                dst_ref=lon_all.at[slab],
+                send_sem=lon_send.at[a],
+                recv_sem=lon_recv.at[a],
+                device_id=(week, lax.rem(slab + a, slabs), trank, lrank),
+                device_id_type=MESH,
+            )
+        )
+        lon_copies[-1].start()
+    meta_copies = []
+    for n, k in enumerate(pieces):
+        meta_copies.append(
+            pltpu.make_async_remote_copy(
+                src_ref=meta_mine,
+                dst_ref=meta_all.at[me],
+                send_sem=meta_send.at[n],
+                recv_sem=meta_recv.at[n],
+                device_id=(week, *peer(k)),
+                device_id_type=MESH,
+            )
+        )
+        meta_copies[-1].start()
+    lon_all[slab] = lon_mine[...]
+    meta_all[me] = meta_mine[...]
+
+    half = lax.broadcasted_iota(jnp.int32, (rows, LANES), 1) < BLK
+    for j in range(BLK // per_lane):
+        chunk = tiles_ref[:, j * LANES : (j + 1) * LANES].astype(jnp.float32)
+        turned = pltpu.roll(chunk, BLK, 1)
+        square[pl.ds(per_lane * j, rows, stride=BLK), :] = jnp.where(half, chunk, turned)
+        square[pl.ds(per_lane * j + 1, rows, stride=BLK), :] = jnp.where(half, turned, chunk)
+    for cb in range(RC // BLK):
+        lat_blocks[cb] = lat_ref[:, cb * BLK : (cb + 1) * BLK]
+    for r in range(rows):
+        e, q = r // capacity, r % capacity
+        partials[e, pl.ds(q, lats, stride=capacity), :] = jnp.dot(
+            lat_blocks[blk_ref[r] // dblocks],
+            square[r * BLK : (r + 1) * BLK, :].astype(jnp.bfloat16),
+            preferred_element_type=jnp.float32,
+        )
+
+    for copy in meta_copies:
+        copy.wait()
+
+    def field(k):
+        return jnp.concatenate(
+            [meta_all[i][:, k * rows : (k + 1) * rows] for i in range(devices)], axis=1
+        )
+
+    variable, rank_time, rank_level, alive = field(0), field(1), field(2), field(3)
+    time_hot = (
+        lax.broadcasted_iota(jnp.int32, (RT, total_rows), 0) == rank_time
+    ).astype(jnp.float32).astype(jnp.bfloat16)
+    level_hot = (
+        lax.broadcasted_iota(jnp.int32, (RL, total_rows), 0) == rank_level
+    ).astype(jnp.float32).astype(jnp.bfloat16)
+    time_f = time_factor_ref[...].astype(jnp.float32)
+    time_rows = jnp.concatenate(
+        [jnp.broadcast_to(time_f[t : t + 1], (levels, RT)) for t in range(hours)], axis=0
+    ).astype(jnp.bfloat16)
+    level_f = level_factor_ref[...].astype(jnp.float32)
+    level_rows = jnp.concatenate([level_f] * hours, axis=0).astype(jnp.bfloat16)
+    product = (
+        jnp.dot(time_rows, time_hot, preferred_element_type=jnp.float32)
+        * jnp.dot(level_rows, level_hot, preferred_element_type=jnp.float32)
+        * alive.astype(jnp.float32)
+    )
+    per_var = hours * levels
+    for v in range(V):
+        coef[v * per_var : (v + 1) * per_var, :] = jnp.where(
+            variable == v, product, 0.0
+        ).astype(jnp.bfloat16)
+
+    for copy in lon_copies:
+        copy.wait()
+    sub = lax.broadcasted_iota(jnp.int32, (capacity, LANES), 0)
+    side = lax.broadcasted_iota(jnp.int32, (capacity, LANES), 1) // BLK
+    for e in range(slabs):
+        place = jnp.zeros((capacity, LANES), jnp.int32)
+        for q in range(capacity):
+            place = jnp.where(sub == q, blk_ref[e * capacity + q] % dblocks, place)
+        part = partials[e].reshape(lats, capacity, LANES)
+        spread = jnp.concatenate(
+            [
+                jnp.where((place == per_lane * b + side)[None], part, 0.0)
+                for b in range(dblocks // per_lane)
+            ],
+            axis=2,
+        ).reshape(lats * capacity, depth).astype(jnp.bfloat16)
+        longitudes = lon_all[:, :, e * depth : (e + 1) * depth].reshape(slabs * lon_pad, depth)
+        value = lax.dot_general(
+            spread, longitudes, (((1,), (1,)), ((), ())), preferred_element_type=jnp.float32
+        )
+        weights[:, :, e * capacity : (e + 1) * capacity, :] = value.reshape(
+            groups, lat_dev, capacity, slabs * lon_pad
+        )
+    for g in range(groups):
+        turned = weights[g].reshape(lat_dev * rows, slabs * lon_pad).T
+        send_buf[g] = turned.astype(jnp.bfloat16).reshape(slabs, lon_pad, lat_dev * rows)
+
+    w_copies = []
+    for n, k in enumerate(pieces):
+        to_slab, to_trank, to_lrank = peer(k)
+        w_copies.append(
+            pltpu.make_async_remote_copy(
+                src_ref=send_buf.at[to_trank * lranks + to_lrank, to_slab],
+                dst_ref=recv_buf.at[me],
+                send_sem=w_send.at[n],
+                recv_sem=w_recv.at[n],
+                device_id=(week, to_slab, to_trank, to_lrank),
+                device_id_type=MESH,
+            )
+        )
+        w_copies[-1].start()
+    recv_buf[me] = send_buf[trank * lranks + lrank, slab]
+    for copy in w_copies:
+        copy.wait()
+
+    got = [recv_buf[i].astype(jnp.float32) for i in range(devices)]
+    left = jnp.concatenate(
+        [
+            jnp.concatenate([x[:, y * rows : (y + 1) * rows] for x in got], axis=1)
+            for y in range(lat_dev)
+        ],
+        axis=0,
+    ).astype(jnp.bfloat16)
+    full = lax.dot_general(
+        left, coef[...], (((1,), (1,)), ((), ())), preferred_element_type=jnp.float32
+    )
+    blocks = full.shape[1] // LANES
+    for b in range(blocks):
+        result[b] = full[:, b * LANES : (b + 1) * LANES]
+    for o in range(lons):
+        out_ref[o] = jnp.concatenate(
+            [result[b, pl.ds(o, lat_dev, stride=lon_pad), :] for b in range(blocks)], axis=1
+        ).astype(jnp.bfloat16)
+
+
+def scratch_of(shape, tiles, lat_factor, lon_factor, fields):
+    slabs, tranks, lranks = shape
+    groups = tranks * lranks
+    devices = slabs * groups
+    rows = tiles.shape[0]
+    lats, lons = lat_factor.shape[0], lon_factor.shape[0]
+    lat_dev = lats // groups
+    lon_pad = -(-lons // 16) * 16
+    return [
+        ((rows * BLK, LANES), jnp.float32),
+        ((RC // BLK, lats, BLK), jnp.bfloat16),
+        ((slabs, lats * (rows // slabs), LANES), jnp.float32),
+        ((lon_pad, RD), jnp.bfloat16),
+        ((slabs, lon_pad, RD), jnp.bfloat16),
+        ((groups, lat_dev, rows, slabs * lon_pad), jnp.float32),
+        ((groups, slabs, lon_pad, lat_dev * rows), jnp.bfloat16),
+        ((devices, lon_pad, lat_dev * rows), jnp.bfloat16),
+        ((1, 4 * rows), jnp.int32),
+        ((devices, 1, 4 * rows), jnp.int32),
+        ((fields, devices * rows), jnp.bfloat16),
+        ((fields // LANES, lat_dev * lon_pad, LANES), jnp.float32),
+    ]
+
+
+def bytes_of(buffers):
+    total = 0
+    for dims, kind in buffers:
+        size = jnp.dtype(kind).itemsize
+        for d in dims[:-1]:
+            size *= d
+        total += size * (-(-dims[-1] // LANES) * LANES)
+    return total
+
+
+def per_device(
+    tiles,
+    tile_var,
+    tile_time,
+    tile_level,
+    tile_block,
+    counts,
+    time_factor,
+    level_factor,
+    lat_factor,
+    lon_factor,
+):
+    shape = tuple(lax.axis_size(name) for name in ("slab", "trank", "lrank"))
+    slabs = shape[0]
+    devices = shape[0] * shape[1] * shape[2]
+    rows = tiles.shape[0]
+    fields = V * time_factor.shape[0] * level_factor.shape[0]
+    buffers = scratch_of(shape, tiles, lat_factor, lon_factor, fields)
+    fits = (
+        4 * rows == LANES
+        and rows // slabs == 8
+        and (RD // slabs) % LANES == 0
+        and fields % LANES == 0
+        and bytes_of(buffers) < (24 << 20)
+    )
+    if not fits:
+        return general_plan(
+            tiles,
+            tile_var,
+            tile_time,
+            tile_level,
+            tile_block,
+            counts,
+            time_factor,
+            level_factor,
+            lat_factor,
+            lon_factor,
+        )
+    lat_dev = lat_factor.shape[0] // (devices // slabs)
+    in_vmem = pl.BlockSpec(memory_space=pltpu.VMEM)
+    in_smem = pl.BlockSpec(memory_space=pltpu.SMEM)
+    return pl.pallas_call(
+        functools.partial(decode_kernel, shape),
+        out_shape=jax.ShapeDtypeStruct((lon_factor.shape[0], lat_dev, fields), jnp.bfloat16),
+        in_specs=[in_vmem] * 4 + [in_smem] * 2 + [in_vmem] * 4,
+        out_specs=in_vmem,
+        scratch_shapes=[pltpu.VMEM(dims, kind) for dims, kind in buffers]
+        + [pltpu.SemaphoreType.DMA((slabs,))] * 2
+        + [pltpu.SemaphoreType.DMA((devices - 1,))] * 4,
+        compiler_params=pltpu.CompilerParams(collective_id=0, has_side_effects=True),
+        name="decode",
+    )(
+        tiles,
+        tile_var.reshape(1, rows),
+        tile_time.reshape(1, rows),
+        tile_level.reshape(1, rows),
+        tile_block,
+        counts,
+        time_factor,
+        level_factor,
+        lat_factor,
+        lon_factor,
+    )
+
+
 def solution(mesh):
     in_specs = (
         P(("week", "slab", "trank", "lrank"), None),

time: 412 us -> 24.2 us (0.06)
  waiting for transfers between devices: 342 us -> 0 us
  starting transfers between devices: 24.5 us -> 0 us
  Pallas kernels: 0 us -> 22.5 us
  between operations: 13.6 us -> 0.01 us
  matrix products: 13.1 us -> 0 us
  local copies, waits for them, and re-layouts: 13.4 us -> 1.52 us
    all_gather x1 -> x0, waiting for transfers between devices: 220 us -> none  [per_device(): lax.all_gather(summed, 'slab', axis=1, tiled=True)]
    reduce_scatter x1 -> x0, waiting for transfers between devices: 99.5 us -> none  [per_device(): lax.psum_scatter(jnp.einsum('kld,kx->ldx', spread, coef, preferred_elemen...]
    all_to_all x6 -> x0, starting transfers between devices: 24.5 us -> none  [the longest x1 6.35 us: per_device(): lax.all_to_all(tile_block, 'slab', split_axis=0, concat_axis=0, tiled=True)]
    all_to_all x6 -> x0, waiting for transfers between devices: 23.2 us -> none  [the longest x1 5.37 us: per_device(): lax.all_to_all(tile_time, 'slab', split_axis=0, concat_axis=0, tiled=True)]
    pallas_call x0 -> x1, Pallas kernels: none -> 22.5 us  [per_device(): pl.pallas_call(functools.partial(decode_kernel, shape), out_shape=jax.Sha...]
    dot_general x3 -> x0, matrix products: 13.1 us -> none  [the longest x1 6.48 us: per_device(): jnp.einsum('kld,kx->ldx', spread, coef, preferred_element_type=jnp.float32)]
    all_to_all x7 -> x0, local copies, waits for them, and re-layouts: 5.97 us -> none  [the longest x4 2.03 us: per_device(): lax.all_to_all(tile_block, 'slab', split_axis=0, concat_axis=0, tiled=True)]
  transfers between devices with their start and end apart: 8 -> 0, of which waited for: 7 -> 0; matrix products, arithmetic and copies ran while one was open for 2% -> 0% of each run, Pallas kernels for 0% -> 0%
where the time goes in v1:
time: 24.2 us; the launch traced here: 24 us
  Pallas kernels  22.5 us (93%)
  local copies, waits for them, and re-layouts  1.52 us (6%)
    pallas_call x1, Pallas kernels, per_device(): pl.pallas_call(functools.partial(decode_kernel, shape), out_shape=jax.Sha...  22.5 us
    unnamed x1, local copies, waits for them, and re-layouts  1.52 us

profile of v1, /device:TPU:0, one launch (start us, length us, event | category | flops | bytes accessed | tf_op | source)
XLA Modules:
  0.0 24.0 jit_solution(1107974427296761544)
XLA Ops:
  0.0 22.5 %decode.1 = bf16[12,8,384]{2,1,0:T(8,128)(2,1)} custom-call(bf16[32,4096]{1,0:T(8,128)(2,1)} %tiles_ref.1, s32[1,32]{1,0:T(1,128)} %bitcast.3, s32[1,32]{1,0:T(1,128)} %bitcast.4, s32[1,32]{1,0:T(1,128)} %bitcast.5, s32[32]{0:T(128)} %blk_ref.1, s32[1,4]{1,0:T(1,128)} %counts_ref.1, bf16[8,256]{1,0:T(8,128)(2,1)} %time_factor_ref.1, ...), custom_call_target="tpu_custom_call" | custom-call | tf_op jit(solution)/shard_map/decode/pallas_call | solution.py:407
  22.5 1.5 %copy.12 = bf16[12,8,384]{2,1,0:T(8,128)(2,1)} copy(bf16[12,8,384]{2,1,0:T(8,128)(2,1)} %decode.1) | data formatting | bytes 147456

commit v2 on v1

--- a/solution.py
+++ b/solution.py
@@ -104,21 +104,24 @@
 
 def decode_kernel(
     shape,
-    tiles_ref,
-    var_ref,
-    time_ref,
-    level_ref,
-    blk_ref,
-    counts_ref,
-    time_factor_ref,
-    level_factor_ref,
-    lat_ref,
-    lon_ref,
+    tiles_hbm,
+    var_hbm,
+    time_hbm,
+    level_hbm,
+    blk_hbm,
+    counts_hbm,
+    time_factor_hbm,
+    level_factor_hbm,
+    lat_hbm,
+    lon_hbm,
     out_ref,
     square,
     lat_blocks,
     partials,
-    lon_mine,
+    stage,
+    stage_place,
+    got_part,
+    got_place,
     lon_all,
     weights,
     send_buf,
@@ -127,8 +130,20 @@
     meta_all,
     coef,
     result,
+    tiles_ref,
+    index_ref,
+    time_factor_ref,
+    level_factor_ref,
+    lat_ref,
+    blk_ref,
+    counts_ref,
+    load_sem,
     lon_send,
     lon_recv,
+    part_send,
+    part_recv,
+    place_send,
+    place_recv,
     meta_send,
     meta_recv,
     w_send,
@@ -146,7 +161,9 @@
     capacity = rows // slabs
     lats = lat_ref.shape[0]
     lat_dev = lats // groups
-    lons, lon_pad = lon_ref.shape[0], lon_mine.shape[0]
+    lons, lon_pad = lon_hbm.shape[0], recv_buf.shape[1]
+    own = slabs // lranks
+    own_rows = own * capacity
     depth = RD // slabs
     dblocks = depth // BLK
     per_lane = LANES // BLK
@@ -165,9 +182,32 @@
             lax.rem(lrank + c, lranks),
         )
 
-    lon_mine[...] = jnp.concatenate(
-        [lon_ref[...].astype(jnp.float32), jnp.zeros((lon_pad - lons, RD), jnp.float32)], axis=0
-    ).astype(jnp.bfloat16)
+    barrier = pltpu.get_barrier_semaphore()
+    for k in pieces:
+        pl.semaphore_signal(barrier, inc=1, device_id=(week, *peer(k)), device_id_type=MESH)
+    columns = pl.ds(pl.multiple_of(lrank * (own * depth), own * depth), own * depth)
+    loads = [
+        pltpu.make_async_copy(src, dst, load_sem.at[n])
+        for n, (src, dst) in enumerate(
+            [
+                (tiles_hbm, tiles_ref),
+                (lat_hbm, lat_ref),
+                (blk_hbm, blk_ref),
+                (counts_hbm, counts_ref),
+                (var_hbm, index_ref.at[0]),
+                (time_hbm, index_ref.at[1]),
+                (level_hbm, index_ref.at[2]),
+                (time_factor_hbm, time_factor_ref),
+                (level_factor_hbm, level_factor_ref),
+                (lon_hbm.at[:, columns], lon_all.at[slab]),
+            ]
+        )
+    ]
+    for load in loads:
+        load.start()
+    for load in loads:
+        load.wait()
+
     lane = lax.broadcasted_iota(jnp.int32, (1, rows), 1)
     live = jnp.zeros((1, rows), jnp.int32)
     for e in range(slabs):
@@ -175,23 +215,20 @@
         live = jnp.where((lane >= first) & (lane < first + counts_ref[0, e]), 1, live)
     meta_mine[...] = jnp.concatenate(
         [
-            var_ref[...],
-            time_ref[...] + trank * time_dev,
-            level_ref[...] + lrank * level_dev,
+            index_ref[0],
+            index_ref[1] + trank * time_dev,
+            index_ref[2] + lrank * level_dev,
             live,
         ],
         axis=1,
     )
-    barrier = pltpu.get_barrier_semaphore()
-    for k in pieces:
-        pl.semaphore_signal(barrier, inc=1, device_id=(week, *peer(k)), device_id_type=MESH)
     pl.semaphore_wait(barrier, devices - 1)
 
     lon_copies = []
     for a in sorted(range(1, slabs), key=lambda a: -min(a, slabs - a)):
         lon_copies.append(
             pltpu.make_async_remote_copy(
-                src_ref=lon_mine,
+                src_ref=lon_hbm.at[:, columns],
                 dst_ref=lon_all.at[slab],
                 send_sem=lon_send.at[a],
                 recv_sem=lon_recv.at[a],
@@ -213,7 +250,6 @@
             )
         )
         meta_copies[-1].start()
-    lon_all[slab] = lon_mine[...]
     meta_all[me] = meta_mine[...]
 
     half = lax.broadcasted_iota(jnp.int32, (rows, LANES), 1) < BLK
@@ -232,12 +268,97 @@
             preferred_element_type=jnp.float32,
         )
 
+    sub = lax.broadcasted_iota(jnp.int32, (capacity, LANES), 0)
+    side = lax.broadcasted_iota(jnp.int32, (capacity, LANES), 1) // BLK
+    for e in range(slabs):
+        place = jnp.zeros((capacity, LANES), jnp.int32)
+        for q in range(capacity):
+            place = jnp.where(sub == q, blk_ref[e * capacity + q] % dblocks, place)
+        stage_place[e] = place
+    stage[...] = partials[...].astype(jnp.bfloat16)
+
+    part_copies = []
+    for c in range(1, lranks):
+        other = lax.rem(lrank + c, lranks)
+        theirs = pl.ds(other * own, own)
+        for src, dst, send, recv in (
+            (stage, got_part, part_send, part_recv),
+            (stage_place, got_place, place_send, place_recv),
+        ):
+            part_copies.append(
+                pltpu.make_async_remote_copy(
+                    src_ref=src.at[theirs],
+                    dst_ref=dst.at[lrank],
+                    send_sem=send.at[c],
+                    recv_sem=recv.at[c],
+                    device_id=(week, slab, trank, other),
+                    device_id_type=MESH,
+                )
+            )
+            part_copies[-1].start()
+    got_part[lrank] = stage[pl.ds(lrank * own, own)]
+    got_place[lrank] = stage_place[pl.ds(lrank * own, own)]
+    for copy in part_copies:
+        copy.wait()
+
+    for copy in lon_copies:
+        copy.wait()
+    blank = jnp.zeros((slabs, lon_pad - lons, depth), jnp.float32)
+    for e in range(own):
+        longitudes = jnp.concatenate(
+            [lon_all[:, :, e * depth : (e + 1) * depth].astype(jnp.float32), blank], axis=1
+        ).reshape(slabs * lon_pad, depth).astype(jnp.bfloat16)
+        for source in range(lranks):
+            place = got_place[source, e]
+            part = got_part[source, e].astype(jnp.float32).reshape(lats, capacity, LANES)
+            spread = jnp.concatenate(
+                [
+                    jnp.where((place == per_lane * b + side)[None], part, 0.0)
+                    for b in range(dblocks // per_lane)
+                ],
+                axis=2,
+            ).reshape(lats * capacity, depth).astype(jnp.bfloat16)
+            value = lax.dot_general(
+                spread, longitudes, (((1,), (1,)), ((), ())), preferred_element_type=jnp.float32
+            )
+            first = source * own_rows + e * capacity
+            weights[:, :, first : first + capacity, :] = value.reshape(
+                groups, lat_dev, capacity, slabs * lon_pad
+            )
+    for g in range(groups):
+        turned = weights[g].reshape(lat_dev * rows, slabs * lon_pad).T
+        send_buf[g] = turned.astype(jnp.bfloat16).reshape(slabs, lon_pad, lat_dev * rows)
+
+    w_copies = []
+    for n, k in enumerate(pieces):
+        to_slab, to_trank, to_lrank = peer(k)
+        w_copies.append(
+            pltpu.make_async_remote_copy(
+                src_ref=send_buf.at[to_trank * lranks + to_lrank, to_slab],
+                dst_ref=recv_buf.at[me],
+                send_sem=w_send.at[n],
+                recv_sem=w_recv.at[n],
+                device_id=(week, to_slab, to_trank, to_lrank),
+                device_id_type=MESH,
+            )
+        )
+        w_copies[-1].start()
+    recv_buf[me] = send_buf[trank * lranks + lrank, slab]
+
     for copy in meta_copies:
         copy.wait()
 
     def field(k):
         return jnp.concatenate(
-            [meta_all[i][:, k * rows : (k + 1) * rows] for i in range(devices)], axis=1
+            [
+                meta_all[p * lranks + source][
+                    :, k * rows + core * own_rows : k * rows + (core + 1) * own_rows
+                ]
+                for p in range(devices // lranks)
+                for core in range(lranks)
+                for source in range(lranks)
+            ],
+            axis=1,
         )
 
     variable, rank_time, rank_level, alive = field(0), field(1), field(2), field(3)
@@ -264,48 +385,6 @@
             variable == v, product, 0.0
         ).astype(jnp.bfloat16)
 
-    for copy in lon_copies:
-        copy.wait()
-    sub = lax.broadcasted_iota(jnp.int32, (capacity, LANES), 0)
-    side = lax.broadcasted_iota(jnp.int32, (capacity, LANES), 1) // BLK
-    for e in range(slabs):
-        place = jnp.zeros((capacity, LANES), jnp.int32)
-        for q in range(capacity):
-            place = jnp.where(sub == q, blk_ref[e * capacity + q] % dblocks, place)
-        part = partials[e].reshape(lats, capacity, LANES)
-        spread = jnp.concatenate(
-            [
-                jnp.where((place == per_lane * b + side)[None], part, 0.0)
-                for b in range(dblocks // per_lane)
-            ],
-            axis=2,
-        ).reshape(lats * capacity, depth).astype(jnp.bfloat16)
-        longitudes = lon_all[:, :, e * depth : (e + 1) * depth].reshape(slabs * lon_pad, depth)
-        value = lax.dot_general(
-            spread, longitudes, (((1,), (1,)), ((), ())), preferred_element_type=jnp.float32
-        )
-        weights[:, :, e * capacity : (e + 1) * capacity, :] = value.reshape(
-            groups, lat_dev, capacity, slabs * lon_pad
-        )
-    for g in range(groups):
-        turned = weights[g].reshape(lat_dev * rows, slabs * lon_pad).T
-        send_buf[g] = turned.astype(jnp.bfloat16).reshape(slabs, lon_pad, lat_dev * rows)
-
-    w_copies = []
-    for n, k in enumerate(pieces):
-        to_slab, to_trank, to_lrank = peer(k)
-        w_copies.append(
-            pltpu.make_async_remote_copy(
-                src_ref=send_buf.at[to_trank * lranks + to_lrank, to_slab],
-                dst_ref=recv_buf.at[me],
-                send_sem=w_send.at[n],
-                recv_sem=w_recv.at[n],
-                device_id=(week, to_slab, to_trank, to_lrank),
-                device_id_type=MESH,
-            )
-        )
-        w_copies[-1].start()
-    recv_buf[me] = send_buf[trank * lranks + lrank, slab]
     for copy in w_copies:
         copy.wait()
 
@@ -329,7 +408,7 @@
         ).astype(jnp.bfloat16)
 
 
-def scratch_of(shape, tiles, lat_factor, lon_factor, fields):
+def scratch_of(shape, tiles, time_factor, level_factor, lat_factor, lon_factor):
     slabs, tranks, lranks = shape
     groups = tranks * lranks
     devices = slabs * groups
@@ -337,12 +416,16 @@
     lats, lons = lat_factor.shape[0], lon_factor.shape[0]
     lat_dev = lats // groups
     lon_pad = -(-lons // 16) * 16
+    fields = V * time_factor.shape[0] * level_factor.shape[0]
     return [
         ((rows * BLK, LANES), jnp.float32),
         ((RC // BLK, lats, BLK), jnp.bfloat16),
         ((slabs, lats * (rows // slabs), LANES), jnp.float32),
-        ((lon_pad, RD), jnp.bfloat16),
-        ((slabs, lon_pad, RD), jnp.bfloat16),
+        ((slabs, lats * (rows // slabs), LANES), jnp.bfloat16),
+        ((slabs, rows // slabs, LANES), jnp.int32),
+        ((lranks, slabs // lranks, lats * (rows // slabs), LANES), jnp.bfloat16),
+        ((lranks, slabs // lranks, rows // slabs, LANES), jnp.int32),
+        ((slabs, lons, RD // lranks), jnp.bfloat16),
         ((groups, lat_dev, rows, slabs * lon_pad), jnp.float32),
         ((groups, slabs, lon_pad, lat_dev * rows), jnp.bfloat16),
         ((devices, lon_pad, lat_dev * rows), jnp.bfloat16),
@@ -350,6 +433,11 @@
         ((devices, 1, 4 * rows), jnp.int32),
         ((fields, devices * rows), jnp.bfloat16),
         ((fields // LANES, lat_dev * lon_pad, LANES), jnp.float32),
+        (tiles.shape, jnp.bfloat16),
+        ((3, 1, rows), jnp.int32),
+        (time_factor.shape, jnp.bfloat16),
+        (level_factor.shape, jnp.bfloat16),
+        (lat_factor.shape, jnp.bfloat16),
     ]
 
 
@@ -380,10 +468,11 @@
     devices = shape[0] * shape[1] * shape[2]
     rows = tiles.shape[0]
     fields = V * time_factor.shape[0] * level_factor.shape[0]
-    buffers = scratch_of(shape, tiles, lat_factor, lon_factor, fields)
+    buffers = scratch_of(shape, tiles, time_factor, level_factor, lat_factor, lon_factor)
     fits = (
         4 * rows == LANES
         and rows // slabs == 8
+        and slabs % shape[2] == 0
         and (RD // slabs) % LANES == 0
         and fields % LANES == 0
         and bytes_of(buffers) < (24 << 20)
@@ -403,14 +492,20 @@
         )
     lat_dev = lat_factor.shape[0] // (devices // slabs)
     in_vmem = pl.BlockSpec(memory_space=pltpu.VMEM)
-    in_smem = pl.BlockSpec(memory_space=pltpu.SMEM)
+    in_hbm = pl.BlockSpec(memory_space=pltpu.HBM)
     return pl.pallas_call(
         functools.partial(decode_kernel, shape),
         out_shape=jax.ShapeDtypeStruct((lon_factor.shape[0], lat_dev, fields), jnp.bfloat16),
-        in_specs=[in_vmem] * 4 + [in_smem] * 2 + [in_vmem] * 4,
+        in_specs=[in_hbm] * 10,
         out_specs=in_vmem,
         scratch_shapes=[pltpu.VMEM(dims, kind) for dims, kind in buffers]
+        + [
+            pltpu.SMEM((rows,), jnp.int32),
+            pltpu.SMEM((1, slabs), jnp.int32),
+            pltpu.SemaphoreType.DMA((10,)),
+        ]
         + [pltpu.SemaphoreType.DMA((slabs,))] * 2
+        + [pltpu.SemaphoreType.DMA((shape[2],))] * 4
         + [pltpu.SemaphoreType.DMA((devices - 1,))] * 4,
         compiler_params=pltpu.CompilerParams(collective_id=0, has_side_effects=True),
         name="decode",

time: 24.2 us -> 19.7 us (0.81)
  Pallas kernels: 22.5 us -> 18 us
    pallas_call x1, Pallas kernels: 22.5 us -> 18 us  [per_device(): pl.pallas_call(functools.partial(decode_kernel, shape), out_shape=jax.Sha...]
where the time goes in v2:
time: 19.7 us; the launch traced here: 19.5 us
  Pallas kernels  18 us (91%)
  local copies, waits for them, and re-layouts  1.52 us (8%)
    pallas_call x1, Pallas kernels, per_device(): pl.pallas_call(functools.partial(decode_kernel, shape), out_shape=jax.Sha...  18 us
    unnamed x1, local copies, waits for them, and re-layouts  1.52 us

profile of v2, /device:TPU:0, one launch (start us, length us, event | category | flops | bytes accessed | tf_op | source)
XLA Modules:
  0.0 19.5 jit_solution(11296258919044326491)
XLA Ops:
  0.0 18.0 %decode.1 = bf16[12,8,384]{2,1,0:T(8,128)(2,1)} custom-call(bf16[32,4096]{1,0:T(8,128)(2,1)} %tiles_hbm.1, s32[1,32]{1,0:T(1,128)} %bitcast.3, s32[1,32]{1,0:T(1,128)} %bitcast.4, s32[1,32]{1,0:T(1,128)} %bitcast.5, s32[32]{0:T(128)} %blk_hbm.1, s32[1,4]{1,0:T(1,128)} %counts_hbm.1, bf16[8,256]{1,0:T(8,128)(2,1)} %time_factor_hbm.1, ...), custom_call_target="tpu_custom_call" | custom-call | tf_op jit(solution)/shard_map/decode/pallas_call | solution.py:496
  18.0 1.5 %copy.12 = bf16[12,8,384]{2,1,0:T(8,128)(2,1)} copy(bf16[12,8,384]{2,1,0:T(8,128)(2,1)} %decode.1) | data formatting | bytes 147456

commit v3 on v2

--- a/solution.py
+++ b/solution.py
@@ -182,6 +182,14 @@
             lax.rem(lrank + c, lranks),
         )
 
+    orders = [sorted(range(slabs), key=lambda t: -abs(t - at)) for at in range(slabs)]
+    line = []
+    for n in range(slabs):
+        target = jnp.int32(orders[0][n])
+        for at in range(1, slabs):
+            target = jnp.where(slab == at, orders[at][n], target)
+        line.append(target)
+
     barrier = pltpu.get_barrier_semaphore()
     for k in pieces:
         pl.semaphore_signal(barrier, inc=1, device_id=(week, *peer(k)), device_id_type=MESH)
@@ -225,14 +233,15 @@
     pl.semaphore_wait(barrier, devices - 1)
 
     lon_copies = []
-    for a in sorted(range(1, slabs), key=lambda a: -min(a, slabs - a)):
+    for to_slab in line[:-1]:
+        a = lax.rem(to_slab - slab + slabs, slabs)
         lon_copies.append(
             pltpu.make_async_remote_copy(
                 src_ref=lon_hbm.at[:, columns],
                 dst_ref=lon_all.at[slab],
                 send_sem=lon_send.at[a],
                 recv_sem=lon_recv.at[a],
-                device_id=(week, lax.rem(slab + a, slabs), trank, lrank),
+                device_id=(week, to_slab, trank, lrank),
                 device_id_type=MESH,
             )
         )
@@ -330,19 +339,26 @@
         send_buf[g] = turned.astype(jnp.bfloat16).reshape(slabs, lon_pad, lat_dev * rows)
 
     w_copies = []
-    for n, k in enumerate(pieces):
-        to_slab, to_trank, to_lrank = peer(k)
-        w_copies.append(
-            pltpu.make_async_remote_copy(
-                src_ref=send_buf.at[to_trank * lranks + to_lrank, to_slab],
-                dst_ref=recv_buf.at[me],
-                send_sem=w_send.at[n],
-                recv_sem=w_recv.at[n],
-                device_id=(week, to_slab, to_trank, to_lrank),
-                device_id_type=MESH,
+    around = sorted(
+        [(b, c) for b in range(tranks) for c in range(lranks)], key=lambda k: -(k[0] * 2 + k[1])
+    )
+    for n, to_slab in enumerate(line):
+        for b, c in around:
+            if n == slabs - 1 and (b, c) == (0, 0):
+                continue
+            _, to_trank, to_lrank = peer((0, b, c))
+            way = lax.rem(to_slab - slab + slabs, slabs) * groups + b * lranks + c
+            w_copies.append(
+                pltpu.make_async_remote_copy(
+                    src_ref=send_buf.at[to_trank * lranks + to_lrank, to_slab],
+                    dst_ref=recv_buf.at[me],
+                    send_sem=w_send.at[way],
+                    recv_sem=w_recv.at[way],
+                    device_id=(week, to_slab, to_trank, to_lrank),
+                    device_id_type=MESH,
+                )
             )
-        )
-        w_copies[-1].start()
+            w_copies[-1].start()
     recv_buf[me] = send_buf[trank * lranks + lrank, slab]
 
     for copy in meta_copies:
@@ -493,6 +509,7 @@
     lat_dev = lat_factor.shape[0] // (devices // slabs)
     in_vmem = pl.BlockSpec(memory_space=pltpu.VMEM)
     in_hbm = pl.BlockSpec(memory_space=pltpu.HBM)
+    hbm = lambda x: pltpu.with_memory_space_constraint(x, pltpu.HBM)
     return pl.pallas_call(
         functools.partial(decode_kernel, shape),
         out_shape=jax.ShapeDtypeStruct((lon_factor.shape[0], lat_dev, fields), jnp.bfloat16),
@@ -506,20 +523,20 @@
         ]
         + [pltpu.SemaphoreType.DMA((slabs,))] * 2
         + [pltpu.SemaphoreType.DMA((shape[2],))] * 4
-        + [pltpu.SemaphoreType.DMA((devices - 1,))] * 4,
-        compiler_params=pltpu.CompilerParams(collective_id=0, has_side_effects=True),
+        + [pltpu.SemaphoreType.DMA((devices,))] * 4,
+        compiler_params=pltpu.CompilerParams(collective_id=0, has_side_effects=True, vmem_limit_bytes=16 << 20),
         name="decode",
     )(
-        tiles,
-        tile_var.reshape(1, rows),
-        tile_time.reshape(1, rows),
-        tile_level.reshape(1, rows),
-        tile_block,
-        counts,
-        time_factor,
-        level_factor,
-        lat_factor,
-        lon_factor,
+        hbm(tiles),
+        hbm(tile_var.reshape(1, rows)),
+        hbm(tile_time.reshape(1, rows)),
+        hbm(tile_level.reshape(1, rows)),
+        hbm(tile_block),
+        hbm(counts),
+        hbm(time_factor),
+        hbm(level_factor),
+        hbm(lat_factor),
+        hbm(lon_factor),
     )
 
 

time: 19.7 us -> 17.2 us (0.87)
  Pallas kernels: 18 us -> 16.4 us
  local copies, waits for them, and re-layouts: 1.52 us -> 0.64 us
    pallas_call x1, Pallas kernels: 18 us -> 16.4 us  [per_device(): pl.pallas_call(functools.partial(decode_kernel, shape), out_shape=jax.Sha...]
    unnamed x1, local copies, waits for them, and re-layouts: 1.52 us -> 0.64 us
where the time goes in v3:
time: 17.2 us; the launch traced here: 17.1 us
  Pallas kernels  16.4 us (95%)
  local copies, waits for them, and re-layouts  0.64 us (4%)
    pallas_call x1, Pallas kernels, per_device(): pl.pallas_call(functools.partial(decode_kernel, shape), out_shape=jax.Sha...  16.4 us
    unnamed x1, local copies, waits for them, and re-layouts  0.64 us

profile of v3, /device:TPU:0, one launch (start us, length us, event | category | flops | bytes accessed | tf_op | source)
XLA Modules:
  0.0 17.1 jit_solution(14866982254625664391)
XLA Ops:
  0.0 16.4 %decode.1 = bf16[12,8,384]{2,1,0:T(8,128)(2,1)S(1)} custom-call(bf16[32,4096]{1,0:T(8,128)(2,1)} %tiles_hbm.1, s32[1,32]{1,0:T(1,128)} %bitcast.3, s32[1,32]{1,0:T(1,128)} %bitcast.4, s32[1,32]{1,0:T(1,128)} %bitcast.5, s32[32]{0:T(128)} %blk_hbm.1, s32[1,4]{1,0:T(1,128)} %counts_hbm.1, bf16[8,256]{1,0:T(8,128)(2,1)} %time_factor_hbm.1, ...), custom_call_target="tpu_custom_call" | custom-call | tf_op jit(solution)/shard_map/decode/pallas_call | solution.py:513
  16.4 0.6 %copy.12 = bf16[12,8,384]{2,1,0:T(8,128)(2,1)} copy(bf16[12,8,384]{2,1,0:T(8,128)(2,1)S(1)} %decode.1) | data formatting | bytes 147456
